TPU v7x, 32 devices: a whole 2x2x4 slice. The times are simulated.
32 devices in a mesh: row: 8 (over y, x, core), col: 4 (over z).
Axes of the slice: x: 2, y: 2, z: 4, core: 2. Of those that a mesh axis runs over, the one named last changes fastest.
Arguments:
- coefficients: float32 [6, 6, 2048, 2048], P(None, None, 'row', 'col'), may hold values from -6 to 6
Outputs:
- convergence: float32 [6, 2048, 2048], P(None, 'row', 'col')
All inputs are finite; a program needn't handle non-finite values.
Results may differ from a plain program's by a relative error of at most 0.00002.
Values sent between devices are 32-bit elements; how exact they have to be, the bound alone decides.
A program may use at most 192 MiB of HBM per device.

v0:
```python
import jax
import jax.numpy as jnp
from jax import lax
from jax.sharding import PartitionSpec as P

SCALES = 5


TAPS = (0.0625, 0.25, 0.375, 0.25, 0.0625)


def with_halo(cells, sides, width):
    for axis, dim in sides:
        count = lax.axis_size(axis)
        ends = count - 1
        head = lax.slice_in_dim(cells, 0, width, axis=dim)
        tail = lax.slice_in_dim(cells, cells.shape[dim] - width, cells.shape[dim], axis=dim)
        cells = jnp.concatenate(
            [
                lax.ppermute(tail, axis, [(i, (i + 1) % count) for i in range(ends)]),
                cells,
                lax.ppermute(head, axis, [((i + 1) % count, i) for i in range(ends)]),
            ],
            axis=dim,
        )
    return cells


def dilated_filter(values, axis, step):
    count = values.shape[axis] - 4 * step
    total = TAPS[0] * lax.slice_in_dim(values, 0, count, axis=axis)
    for k in range(1, 5):
        total = total + TAPS[k] * lax.slice_in_dim(values, k * step, k * step + count, axis=axis)
    return total


def on_device(coefficients):
    field = coefficients[SCALES]
    for j in reversed(range(SCALES)):
        step = 2**j
        plane = coefficients[j]
        change = field - plane
        padded = with_halo(change, (("row", 1),), 2 * step)
        filtered = dilated_filter(padded, 1, step)
        padded = with_halo(filtered, (("col", 2),), 2 * step)
        filtered = dilated_filter(padded, 2, step)
        field = plane + filtered
    return field


def solution(mesh):
    return jax.shard_map(
        on_device,
        mesh=mesh,
        in_specs=(P(None, None, "row", "col"),),
        out_specs=P(None, "row", "col"),
        check_vma=False,
    )
```

profile of v0, /device:TPU:4, one launch (start us, length us, event | category | flops | bytes accessed | tf_op | source)
XLA Modules:
  0.0 174.4 jit_solution(14608640734725655664)
XLA Ops:
  0.0 3.6 %bitcast_subtract_fusion = f32[6,256,512]{2,1,0:T(8,128)S(1)} fusion(f32[6,6,256,512]{3,2,1,0:T(8,128)} %param.1), kind=kLoop, calls=%fused_computation.169 | loop fusion | flops 786432 | bytes 9437184 | tf_op jit(solution)/shard_map/sub | solution.py:42
  5.6 4.5 %collective-permute-start.1 = (f32[6,32,512]{2,1,0:T(8,128)S(1)}, f32[6,32,512]{2,1,0:T(8,128)S(1)}, u32[]{:S(2)}, u32[]{:S(2)}) collective-permute-start(f32[6,32,512]{2,1,0:T(8,128)S(1)} %get-tuple-element.24), channel_id=1, source_target_pairs={{4,0},{8,4},{12,8},{16,12},{20,16},{24,20},{28,24},{5,1},{9,5},{13... | collective-permute-start | bytes 1179656 | tf_op jit(solution)/shard_map/ppermute | solution.py:22
  10.1 4.9 %collective-permute-done = f32[6,32,512]{2,1,0:T(8,128)S(1)} collective-permute-done((f32[6,32,512]{2,1,0:T(8,128)S(1)}, f32[6,32,512]{2,1,0:T(8,128)S(1)}, u32[]{:S(2)}, u32[]{:S(2)}) %collective-permute-start) | collective-permute-done | bytes 393248 | tf_op jit(solution)/shard_map/ppermute | solution.py:20
  16.0 2.0 %fusion.35 = f32[6,256,512]{2,1,0:T(8,128)S(1)} fusion(f32[6,256,512]{2,1,0:T(8,128)S(1)} %bitcast_subtract_fusion, f32[6,32,512]{2,1,0:T(8,128)S(1)} %collective-permute-done.1, f32[6,32,512]{2,1,0:T(8,128)S(1)} %collective-permute-done), kind=kLoop, calls=%fused_computation.75 | loop fusion | flops 10223616 | bytes 7077888 | tf_op jit(solution)/shard_map/add | solution.py:33
  20.7 3.5 %collective-permute-start.2 = (f32[6,256,32]{1,2,0:T(8,128)S(1)}, f32[6,256,32]{1,2,0:T(8,128)S(1)}, u32[]{:S(2)}, u32[]{:S(2)}) collective-permute-start(f32[6,256,32]{1,2,0:T(8,128)S(1)} %copy.17), channel_id=1, source_target_pairs={{0,1},{1,2},{2,3},{4,5},{5,6},{6,7},{8,9},{9,10},{10,11},{12,13},{... | collective-permute-start | bytes 589832 | tf_op jit(solution)/shard_map/ppermute | solution.py:20
  24.2 2.1 %copy.19 = f32[6,256,32]{1,2,0:T(8,128)} copy(f32[6,256,32]{2,1,0:T(8,128)} %get-tuple-element.22) | data formatting | bytes 393216 | tf_op jit(solution)/shard_map/slice | solution.py:16
  30.0 5.3 %collective-permute-done.3 = f32[6,256,32]{1,2,0:T(8,128)} collective-permute-done((f32[6,256,32]{1,2,0:T(8,128)}, f32[6,256,32]{1,2,0:T(8,128)}, u32[]{:S(2)}, u32[]{:S(2)}) %collective-permute-start.3) | collective-permute-done | bytes 196640 | tf_op jit(solution)/shard_map/ppermute | solution.py:22
  35.3 2.1 %copy.20 = f32[6,256,32]{2,1,0:T(8,128)} copy(f32[6,256,32]{1,2,0:T(8,128)} %collective-permute-done.3) | data formatting | bytes 393216 | tf_op jit(solution)/shard_map/ppermute | solution.py:22
  37.4 7.1 %fusion.84 = f32[6,256,512]{2,1,0:T(8,128)S(1)} fusion(f32[6,256,512]{2,1,0:T(8,128)S(1)} %fusion.35, f32[6,256,32]{2,1,0:T(8,128)} %copy.20, f32[6,256,32]{2,1,0:T(8,128)} %copy.18, f32[6,6,256,512]{3,2,1,0:T(8,128)} %param.1), kind=kLoop, calls=%fused_computation.124 | loop fusion | flops 11796480 | bytes 12976128 | tf_op jit(solution)/shard_map/sub | solution.py:42
  44.5 1.9 %collective-permute-start.4 = (f32[6,16,512]{2,1,0:T(8,128)S(1)}, f32[6,16,512]{2,1,0:T(8,128)S(1)}, u32[]{:S(2)}, u32[]{:S(2)}) collective-permute-start(f32[6,16,512]{2,1,0:T(8,128)S(1)} %get-tuple-element.19), channel_id=1, source_target_pairs={{0,4},{4,8},{8,12},{12,16},{16,20},{20,24},{24,28},{1,5},{5,9},{9,... | collective-permute-start | bytes 589832 | tf_op jit(solution)/shard_map/ppermute | solution.py:20
  46.5 4.5 %collective-permute-start.5 = (f32[6,16,512]{2,1,0:T(8,128)S(1)}, f32[6,16,512]{2,1,0:T(8,128)S(1)}, u32[]{:S(2)}, u32[]{:S(2)}) collective-permute-start(f32[6,16,512]{2,1,0:T(8,128)S(1)} %get-tuple-element.20), channel_id=1, source_target_pairs={{4,0},{8,4},{12,8},{16,12},{20,16},{24,20},{28,24},{5,1},{9,5},{13... | collective-permute-start | bytes 589832 | tf_op jit(solution)/shard_map/ppermute | solution.py:22
  54.2 2.0 %fusion.27 = f32[6,256,512]{2,1,0:T(8,128)S(1)} fusion(f32[6,256,512]{2,1,0:T(8,128)S(1)} %fusion.84, f32[6,16,512]{2,1,0:T(8,128)S(1)} %collective-permute-done.5, f32[6,16,512]{2,1,0:T(8,128)S(1)} %collective-permute-done.4), kind=kLoop, calls=%fused_computation.67 | loop fusion | flops 10223616 | bytes 6684672 | tf_op jit(solution)/shard_map/add | solution.py:33
  58.9 3.5 %collective-permute-start.6 = (f32[6,256,16]{1,2,0:T(8,128)S(1)}, f32[6,256,16]{1,2,0:T(8,128)S(1)}, u32[]{:S(2)}, u32[]{:S(2)}) collective-permute-start(f32[6,256,16]{1,2,0:T(8,128)S(1)} %copy.21), channel_id=1, source_target_pairs={{0,1},{1,2},{2,3},{4,5},{5,6},{6,7},{8,9},{9,10},{10,11},{12,13},{... | collective-permute-start | bytes 294920 | tf_op jit(solution)/shard_map/ppermute | solution.py:20
  66.2 4.0 %collective-permute-done.7 = f32[6,256,16]{1,2,0:T(8,128)S(1)} collective-permute-done((f32[6,256,16]{1,2,0:T(8,128)S(1)}, f32[6,256,16]{1,2,0:T(8,128)S(1)}, u32[]{:S(2)}, u32[]{:S(2)}) %collective-permute-start.7) | collective-permute-done | bytes 98336 | tf_op jit(solution)/shard_map/ppermute | solution.py:22
  71.4 7.1 %fusion.74 = f32[6,256,512]{2,1,0:T(8,128)S(1)} fusion(f32[6,256,512]{2,1,0:T(8,128)S(1)} %fusion.27, f32[6,256,16]{2,1,0:T(8,128)} %copy.24, f32[6,256,16]{2,1,0:T(8,128)} %copy.22, f32[6,6,256,512]{3,2,1,0:T(8,128)} %param.1), kind=kLoop, calls=%fused_computation.114 | loop fusion | flops 11796480 | bytes 12779520 | tf_op jit(solution)/shard_map/sub | solution.py:42
  80.5 4.5 %collective-permute-start.9 = (f32[6,8,512]{2,1,0:T(8,128)S(1)}, f32[6,8,512]{2,1,0:T(8,128)S(1)}, u32[]{:S(2)}, u32[]{:S(2)}) collective-permute-start(f32[6,8,512]{2,1,0:T(8,128)S(1)} %get-tuple-element.16), channel_id=1, source_target_pairs={{4,0},{8,4},{12,8},{16,12},{20,16},{24,20},{28,24},{5,1},{9,5},{13... | collective-permute-start | bytes 294920 | tf_op jit(solution)/shard_map/ppermute | solution.py:22
  91.5 3.5 %collective-permute-start.10 = (f32[6,256,8]{1,2,0:T(8,128)S(1)}, f32[6,256,8]{1,2,0:T(8,128)S(1)}, u32[]{:S(2)}, u32[]{:S(2)}) collective-permute-start(f32[6,256,8]{1,2,0:T(8,128)S(1)} %copy.25), channel_id=1, source_target_pairs={{0,1},{1,2},{2,3},{4,5},{5,6},{6,7},{8,9},{9,10},{10,11},{12,13},{... | collective-permute-start | bytes 147464 | tf_op jit(solution)/shard_map/ppermute | solution.py:20
  99.0 3.3 %collective-permute-done.11 = f32[6,256,8]{1,2,0:T(8,128)S(1)} collective-permute-done((f32[6,256,8]{1,2,0:T(8,128)S(1)}, f32[6,256,8]{1,2,0:T(8,128)S(1)}, u32[]{:S(2)}, u32[]{:S(2)}) %collective-permute-start.11) | collective-permute-done | bytes 49184 | tf_op jit(solution)/shard_map/ppermute | solution.py:22
  103.5 7.1 %fusion.64 = f32[6,256,512]{2,1,0:T(8,128)S(1)} fusion(f32[6,256,512]{2,1,0:T(8,128)S(1)} %fusion.19, f32[6,256,8]{2,1,0:T(8,128)} %copy.28, f32[6,256,8]{2,1,0:T(8,128)} %copy.26, f32[6,6,256,512]{3,2,1,0:T(8,128)} %param.1), kind=kLoop, calls=%fused_computation.104 | loop fusion | flops 11796480 | bytes 12681216 | tf_op jit(solution)/shard_map/sub | solution.py:42
  110.6 3.2 %collective-permute-start.13 = (f32[6,4,512]{2,0,1:T(8,128)S(1)}, f32[6,4,512]{2,0,1:T(8,128)S(1)}, u32[]{:S(2)}, u32[]{:S(2)}) collective-permute-start(f32[6,4,512]{2,0,1:T(8,128)S(1)} %copy.31), channel_id=1, source_target_pairs={{4,0},{8,4},{12,8},{16,12},{20,16},{24,20},{28,24},{5,1},{9,5},{13... | collective-permute-start | bytes 147464 | tf_op jit(solution)/shard_map/ppermute | solution.py:22
  113.9 1.9 %collective-permute-start.12 = (f32[6,4,512]{2,0,1:T(8,128)S(1)}, f32[6,4,512]{2,0,1:T(8,128)S(1)}, u32[]{:S(2)}, u32[]{:S(2)}) collective-permute-start(f32[6,4,512]{2,0,1:T(8,128)S(1)} %copy.29), channel_id=1, source_target_pairs={{0,4},{4,8},{8,12},{12,16},{16,20},{20,24},{24,28},{1,5},{5,9},{9,... | collective-permute-start | bytes 147464 | tf_op jit(solution)/shard_map/ppermute | solution.py:20
  115.9 4.4 %collective-permute-done.12 = f32[6,4,512]{2,0,1:T(8,128)S(1)} collective-permute-done((f32[6,4,512]{2,0,1:T(8,128)S(1)}, f32[6,4,512]{2,0,1:T(8,128)S(1)}, u32[]{:S(2)}, u32[]{:S(2)}) %collective-permute-start.12) | collective-permute-done | bytes 49184 | tf_op jit(solution)/shard_map/ppermute | solution.py:20
  120.4 2.0 %fusion.11 = f32[6,256,512]{2,1,0:T(8,128)S(1)} fusion(f32[6,256,512]{2,1,0:T(8,128)S(1)} %fusion.64, f32[6,4,512]{2,1,0:T(4,128)S(1)} %copy.32, f32[6,4,512]{2,1,0:T(4,128)S(1)} %copy.30), kind=kLoop, calls=%fused_computation.51 | loop fusion | flops 10223616 | bytes 6389760 | tf_op jit(solution)/shard_map/add | solution.py:33
  125.3 2.2 %collective-permute-start.14 = (f32[6,256,4]{1,0,2:T(8,128)S(1)}, f32[6,256,4]{1,0,2:T(8,128)S(1)}, u32[]{:S(2)}, u32[]{:S(2)}) collective-permute-start(f32[6,256,4]{1,0,2:T(8,128)S(1)} %copy.33), channel_id=1, source_target_pairs={{0,1},{1,2},{2,3},{4,5},{5,6},{6,7},{8,9},{9,10},{10,11},{12,13},{... | collective-permute-start | bytes 73736 | tf_op jit(solution)/shard_map/ppermute | solution.py:20
  131.5 3.3 %collective-permute-done.15 = f32[6,256,4]{1,0,2:T(8,128)S(1)} collective-permute-done((f32[6,256,4]{1,0,2:T(8,128)S(1)}, f32[6,256,4]{1,0,2:T(8,128)S(1)}, u32[]{:S(2)}, u32[]{:S(2)}) %collective-permute-start.15) | collective-permute-done | bytes 24608 | tf_op jit(solution)/shard_map/ppermute | solution.py:22
  135.9 7.1 %fusion.54 = f32[6,256,512]{2,1,0:T(8,128)S(1)} fusion(f32[6,256,512]{2,1,0:T(8,128)S(1)} %fusion.11, f32[6,256,4]{2,1,0:T(8,128)} %copy.36, f32[6,256,4]{2,1,0:T(8,128)} %copy.34, f32[6,6,256,512]{3,2,1,0:T(8,128)} %param.1), kind=kLoop, calls=%fused_computation.94 | loop fusion | flops 11796480 | bytes 12632064 | tf_op jit(solution)/shard_map/sub | solution.py:42
  145.0 2.4 %collective-permute-start.16 = (f32[6,2,512]{2,0,1:T(8,128)S(1)}, f32[6,2,512]{2,0,1:T(8,128)S(1)}, u32[]{:S(2)}, u32[]{:S(2)}) collective-permute-start(f32[6,2,512]{2,0,1:T(8,128)S(1)} %copy.37), channel_id=1, source_target_pairs={{0,4},{4,8},{8,12},{12,16},{16,20},{20,24},{24,28},{1,5},{5,9},{9,... | collective-permute-start | bytes 73736 | tf_op jit(solution)/shard_map/ppermute | solution.py:20
  147.5 3.7 %collective-permute-done.16 = f32[6,2,512]{2,0,1:T(8,128)S(1)} collective-permute-done((f32[6,2,512]{2,0,1:T(8,128)S(1)}, f32[6,2,512]{2,0,1:T(8,128)S(1)}, u32[]{:S(2)}, u32[]{:S(2)}) %collective-permute-start.16) | collective-permute-done | bytes 24608 | tf_op jit(solution)/shard_map/ppermute | solution.py:20
  151.2 2.0 %fusion.3 = f32[6,256,512]{2,1,0:T(8,128)S(1)} fusion(f32[6,256,512]{2,1,0:T(8,128)S(1)} %fusion.54, f32[6,2,512]{2,1,0:T(2,128)S(1)} %copy.40, f32[6,2,512]{2,1,0:T(2,128)S(1)} %copy.38), kind=kLoop, calls=%fused_computation.43 | loop fusion | flops 10223616 | bytes 6340608 | tf_op jit(solution)/shard_map/add | solution.py:33
  156.1 2.1 %collective-permute-start.18 = (f32[6,256,2]{1,0,2:T(8,128)S(1)}, f32[6,256,2]{1,0,2:T(8,128)S(1)}, u32[]{:S(2)}, u32[]{:S(2)}) collective-permute-start(f32[6,256,2]{1,0,2:T(8,128)S(1)} %copy.41), channel_id=1, source_target_pairs={{0,1},{1,2},{2,3},{4,5},{5,6},{6,7},{8,9},{9,10},{10,11},{12,13},{... | collective-permute-start | bytes 36872 | tf_op jit(solution)/shard_map/ppermute | solution.py:20
  162.4 2.9 %collective-permute-done.19 = f32[6,256,2]{1,0,2:T(8,128)S(1)} collective-permute-done((f32[6,256,2]{1,0,2:T(8,128)S(1)}, f32[6,256,2]{1,0,2:T(8,128)S(1)}, u32[]{:S(2)}, u32[]{:S(2)}) %collective-permute-start.19) | collective-permute-done | bytes 12320 | tf_op jit(solution)/shard_map/ppermute | solution.py:22
  166.5 8.0 %fusion.44 = f32[6,256,512]{2,1,0:T(8,128)} fusion(f32[6,256,512]{2,1,0:T(8,128)S(1)} %fusion.3, f32[6,256,2]{2,1,0:T(8,128)} %copy.44, f32[6,256,2]{2,1,0:T(8,128)} %copy.42, f32[6,6,256,512]{3,2,1,0:T(8,128)} %param.1), kind=kLoop, calls=%fused_computation.84 | loop fusion | flops 11010048 | bytes 9461760 | tf_op jit(solution)/shard_map/add | solution.py:47
  (57 shorter events, 52.3 us)
Async XLA Ops:
  3.7 11.4 %collective-permute-start = (f32[6,32,512]{2,1,0:T(8,128)S(1)}, f32[6,32,512]{2,1,0:T(8,128)S(1)}, u32[]{:S(2)}, u32[]{:S(2)}) collective-permute-start(f32[6,32,512]{2,1,0:T(8,128)S(1)} %get-tuple-element.23), channel_id=1, source_target_pairs={{0,4},{4,8},{8,12},{12,16},{16,20},{20,24},{24,28},{1,5},{5,9},{9,... | collective-permute-start | bytes 1179656 | tf_op jit(solution)/shard_map/ppermute | solution.py:20
  5.6 10.4 %collective-permute-start.1 = (f32[6,32,512]{2,1,0:T(8,128)S(1)}, f32[6,32,512]{2,1,0:T(8,128)S(1)}, u32[]{:S(2)}, u32[]{:S(2)}) collective-permute-start(f32[6,32,512]{2,1,0:T(8,128)S(1)} %get-tuple-element.24), channel_id=1, source_target_pairs={{4,0},{8,4},{12,8},{16,12},{20,16},{24,20},{28,24},{5,1},{9,5},{13... | collective-permute-start | bytes 1179656 | tf_op jit(solution)/shard_map/ppermute | solution.py:22
  20.7 8.1 %collective-permute-start.2 = (f32[6,256,32]{1,2,0:T(8,128)S(1)}, f32[6,256,32]{1,2,0:T(8,128)S(1)}, u32[]{:S(2)}, u32[]{:S(2)}) collective-permute-start(f32[6,256,32]{1,2,0:T(8,128)S(1)} %copy.17), channel_id=1, source_target_pairs={{0,1},{1,2},{2,3},{4,5},{5,6},{6,7},{8,9},{9,10},{10,11},{12,13},{... | collective-permute-start | bytes 589832 | tf_op jit(solution)/shard_map/ppermute | solution.py:20
  26.3 9.0 %collective-permute-start.3 = (f32[6,256,32]{1,2,0:T(8,128)}, f32[6,256,32]{1,2,0:T(8,128)}, u32[]{:S(2)}, u32[]{:S(2)}) collective-permute-start(f32[6,256,32]{1,2,0:T(8,128)} %copy.19), channel_id=1, source_target_pairs={{1,0},{2,1},{3,2},{5,4},{6,5},{7,6},{9,8},{10,9},{11,10},{13,12},{... | collective-permute-start | bytes 589832 | tf_op jit(solution)/shard_map/ppermute | solution.py:22
  44.5 7.9 %collective-permute-start.4 = (f32[6,16,512]{2,1,0:T(8,128)S(1)}, f32[6,16,512]{2,1,0:T(8,128)S(1)}, u32[]{:S(2)}, u32[]{:S(2)}) collective-permute-start(f32[6,16,512]{2,1,0:T(8,128)S(1)} %get-tuple-element.19), channel_id=1, source_target_pairs={{0,4},{4,8},{8,12},{12,16},{16,20},{20,24},{24,28},{1,5},{5,9},{9,... | collective-permute-start | bytes 589832 | tf_op jit(solution)/shard_map/ppermute | solution.py:20
  46.5 7.7 %collective-permute-start.5 = (f32[6,16,512]{2,1,0:T(8,128)S(1)}, f32[6,16,512]{2,1,0:T(8,128)S(1)}, u32[]{:S(2)}, u32[]{:S(2)}) collective-permute-start(f32[6,16,512]{2,1,0:T(8,128)S(1)} %get-tuple-element.20), channel_id=1, source_target_pairs={{4,0},{8,4},{12,8},{16,12},{20,16},{24,20},{28,24},{5,1},{9,5},{13... | collective-permute-start | bytes 589832 | tf_op jit(solution)/shard_map/ppermute | solution.py:22
  58.9 6.2 %collective-permute-start.6 = (f32[6,256,16]{1,2,0:T(8,128)S(1)}, f32[6,256,16]{1,2,0:T(8,128)S(1)}, u32[]{:S(2)}, u32[]{:S(2)}) collective-permute-start(f32[6,256,16]{1,2,0:T(8,128)S(1)} %copy.21), channel_id=1, source_target_pairs={{0,1},{1,2},{2,3},{4,5},{5,6},{6,7},{8,9},{9,10},{10,11},{12,13},{... | collective-permute-start | bytes 294920 | tf_op jit(solution)/shard_map/ppermute | solution.py:20
  63.8 6.5 %collective-permute-start.7 = (f32[6,256,16]{1,2,0:T(8,128)S(1)}, f32[6,256,16]{1,2,0:T(8,128)S(1)}, u32[]{:S(2)}, u32[]{:S(2)}) collective-permute-start(f32[6,256,16]{1,2,0:T(8,128)S(1)} %copy.23), channel_id=1, source_target_pairs={{1,0},{2,1},{3,2},{5,4},{6,5},{7,6},{9,8},{10,9},{11,10},{13,12},{... | collective-permute-start | bytes 294920 | tf_op jit(solution)/shard_map/ppermute | solution.py:22
  78.6 6.8 %collective-permute-start.8 = (f32[6,8,512]{2,1,0:T(8,128)S(1)}, f32[6,8,512]{2,1,0:T(8,128)S(1)}, u32[]{:S(2)}, u32[]{:S(2)}) collective-permute-start(f32[6,8,512]{2,1,0:T(8,128)S(1)} %get-tuple-element.15), channel_id=1, source_target_pairs={{0,4},{4,8},{8,12},{12,16},{16,20},{20,24},{24,28},{1,5},{5,9},{9,... | collective-permute-start | bytes 294920 | tf_op jit(solution)/shard_map/ppermute | solution.py:20
  80.5 6.7 %collective-permute-start.9 = (f32[6,8,512]{2,1,0:T(8,128)S(1)}, f32[6,8,512]{2,1,0:T(8,128)S(1)}, u32[]{:S(2)}, u32[]{:S(2)}) collective-permute-start(f32[6,8,512]{2,1,0:T(8,128)S(1)} %get-tuple-element.16), channel_id=1, source_target_pairs={{4,0},{8,4},{12,8},{16,12},{20,16},{24,20},{28,24},{5,1},{9,5},{13... | collective-permute-start | bytes 294920 | tf_op jit(solution)/shard_map/ppermute | solution.py:22
  91.5 6.3 %collective-permute-start.10 = (f32[6,256,8]{1,2,0:T(8,128)S(1)}, f32[6,256,8]{1,2,0:T(8,128)S(1)}, u32[]{:S(2)}, u32[]{:S(2)}) collective-permute-start(f32[6,256,8]{1,2,0:T(8,128)S(1)} %copy.25), channel_id=1, source_target_pairs={{0,1},{1,2},{2,3},{4,5},{5,6},{6,7},{8,9},{9,10},{10,11},{12,13},{... | collective-permute-start | bytes 147464 | tf_op jit(solution)/shard_map/ppermute | solution.py:20
  96.3 6.0 %collective-permute-start.11 = (f32[6,256,8]{1,2,0:T(8,128)S(1)}, f32[6,256,8]{1,2,0:T(8,128)S(1)}, u32[]{:S(2)}, u32[]{:S(2)}) collective-permute-start(f32[6,256,8]{1,2,0:T(8,128)S(1)} %copy.27), channel_id=1, source_target_pairs={{1,0},{2,1},{3,2},{5,4},{6,5},{7,6},{9,8},{10,9},{11,10},{13,12},{... | collective-permute-start | bytes 147464 | tf_op jit(solution)/shard_map/ppermute | solution.py:22
  110.6 5.3 %collective-permute-start.13 = (f32[6,4,512]{2,0,1:T(8,128)S(1)}, f32[6,4,512]{2,0,1:T(8,128)S(1)}, u32[]{:S(2)}, u32[]{:S(2)}) collective-permute-start(f32[6,4,512]{2,0,1:T(8,128)S(1)} %copy.31), channel_id=1, source_target_pairs={{4,0},{8,4},{12,8},{16,12},{20,16},{24,20},{28,24},{5,1},{9,5},{13... | collective-permute-start | bytes 147464 | tf_op jit(solution)/shard_map/ppermute | solution.py:22
  113.9 6.5 %collective-permute-start.12 = (f32[6,4,512]{2,0,1:T(8,128)S(1)}, f32[6,4,512]{2,0,1:T(8,128)S(1)}, u32[]{:S(2)}, u32[]{:S(2)}) collective-permute-start(f32[6,4,512]{2,0,1:T(8,128)S(1)} %copy.29), channel_id=1, source_target_pairs={{0,4},{4,8},{8,12},{12,16},{16,20},{20,24},{24,28},{1,5},{5,9},{9,... | collective-permute-start | bytes 147464 | tf_op jit(solution)/shard_map/ppermute | solution.py:20
  125.3 5.0 %collective-permute-start.14 = (f32[6,256,4]{1,0,2:T(8,128)S(1)}, f32[6,256,4]{1,0,2:T(8,128)S(1)}, u32[]{:S(2)}, u32[]{:S(2)}) collective-permute-start(f32[6,256,4]{1,0,2:T(8,128)S(1)} %copy.33), channel_id=1, source_target_pairs={{0,1},{1,2},{2,3},{4,5},{5,6},{6,7},{8,9},{9,10},{10,11},{12,13},{... | collective-permute-start | bytes 73736 | tf_op jit(solution)/shard_map/ppermute | solution.py:20
  128.9 5.8 %collective-permute-start.15 = (f32[6,256,4]{1,0,2:T(8,128)S(1)}, f32[6,256,4]{1,0,2:T(8,128)S(1)}, u32[]{:S(2)}, u32[]{:S(2)}) collective-permute-start(f32[6,256,4]{1,0,2:T(8,128)S(1)} %copy.35), channel_id=1, source_target_pairs={{1,0},{2,1},{3,2},{5,4},{6,5},{7,6},{9,8},{10,9},{11,10},{13,12},{... | collective-permute-start | bytes 73736 | tf_op jit(solution)/shard_map/ppermute | solution.py:22
  143.1 4.4 %collective-permute-start.17 = (f32[6,2,512]{2,0,1:T(8,128)S(1)}, f32[6,2,512]{2,0,1:T(8,128)S(1)}, u32[]{:S(2)}, u32[]{:S(2)}) collective-permute-start(f32[6,2,512]{2,0,1:T(8,128)S(1)} %copy.39), channel_id=1, source_target_pairs={{4,0},{8,4},{12,8},{16,12},{20,16},{24,20},{28,24},{5,1},{9,5},{13... | collective-permute-start | bytes 73736 | tf_op jit(solution)/shard_map/ppermute | solution.py:22
  145.0 6.1 %collective-permute-start.16 = (f32[6,2,512]{2,0,1:T(8,128)S(1)}, f32[6,2,512]{2,0,1:T(8,128)S(1)}, u32[]{:S(2)}, u32[]{:S(2)}) collective-permute-start(f32[6,2,512]{2,0,1:T(8,128)S(1)} %copy.37), channel_id=1, source_target_pairs={{0,4},{4,8},{8,12},{12,16},{16,20},{20,24},{24,28},{1,5},{5,9},{9,... | collective-permute-start | bytes 73736 | tf_op jit(solution)/shard_map/ppermute | solution.py:20
  156.1 5.1 %collective-permute-start.18 = (f32[6,256,2]{1,0,2:T(8,128)S(1)}, f32[6,256,2]{1,0,2:T(8,128)S(1)}, u32[]{:S(2)}, u32[]{:S(2)}) collective-permute-start(f32[6,256,2]{1,0,2:T(8,128)S(1)} %copy.41), channel_id=1, source_target_pairs={{0,1},{1,2},{2,3},{4,5},{5,6},{6,7},{8,9},{9,10},{10,11},{12,13},{... | collective-permute-start | bytes 36872 | tf_op jit(solution)/shard_map/ppermute | solution.py:20
  159.6 5.6 %collective-permute-start.19 = (f32[6,256,2]{1,0,2:T(8,128)S(1)}, f32[6,256,2]{1,0,2:T(8,128)S(1)}, u32[]{:S(2)}, u32[]{:S(2)}) collective-permute-start(f32[6,256,2]{1,0,2:T(8,128)S(1)} %copy.43), channel_id=1, source_target_pairs={{1,0},{2,1},{3,2},{5,4},{6,5},{7,6},{9,8},{10,9},{11,10},{13,12},{... | collective-permute-start | bytes 36872 | tf_op jit(solution)/shard_map/ppermute | solution.py:22
where the time goes:
time: 175 us; the launch traced here: 174 us
  starting transfers between devices  50.4 us (29%)
  other arithmetic  49.4 us (28%)
  waiting for transfers between devices  39.5 us (23%)
  local copies, waits for them, and re-layouts  34.7 us (20%)
    sub x5, other arithmetic, on_device(): change = field - plane  32 us
    ppermute x10, starting transfers between devices, with_halo(): lax.ppermute(head, axis, [((i + 1) % count, i) for i in range(ends)])  25.6 us
    ppermute x10, starting transfers between devices, with_halo(): lax.ppermute(tail, axis, [(i, (i + 1) % count) for i in range(ends)])  24.8 us
    ppermute x10, waiting for transfers between devices, with_halo(): lax.ppermute(head, axis, [((i + 1) % count, i) for i in range(ends)])  23.5 us
    ppermute x10, waiting for transfers between devices, with_halo(): lax.ppermute(tail, axis, [(i, (i + 1) % count) for i in range(ends)])  16 us
    slice x17, local copies, waits for them, and re-layouts, with_halo(): lax.slice_in_dim(cells, cells.shape[dim] - width, cells.shape[dim], axis=...  14.2 us
    add x5, other arithmetic, dilated_filter(): total + TAPS[k] * lax.slice_in_dim(values, k * step, k * step + count, ax...  9.44 us
    add x1, other arithmetic, on_device(): field = plane + filtered  7.95 us
  transfers between devices with their start and end apart: 20, of which 15 were waited for; matrix products, arithmetic and copies ran while one was open for 8% of the time, Pallas kernels for 0%

commit v1 on v0

v1 whole, which is shorter than its diff:
```python
import functools

import jax
import jax.numpy as jnp
from jax import lax
from jax.experimental import pallas as pl
from jax.experimental.pallas import tpu as pltpu
from jax.sharding import PartitionSpec as P

SCALES = 5
LANES = 128
STEPS = tuple(2**j for j in range(SCALES))
REACH = tuple(max(2 * s, 8) for s in STEPS)
SCALE = 1.0 / 256.0


def taps(x0, x1, x2, x3, x4):
    return (x0 + x4) + 4.0 * (x1 + x3) + 6.0 * x2


def body(count_row, count_col, coef, out, planes, thin, *scratch):
    diff = scratch[:SCALES]
    sent = scratch[SCALES : 2 * SCALES]
    got = scratch[2 * SCALES : 3 * SCALES]
    load_sem, store_sem, row_send, row_recv, col_send, col_recv = scratch[3 * SCALES :]
    bins, tiles, rows, _ = planes.shape[1:]

    me_row = lax.axis_index("row")
    me_col = lax.axis_index("col")
    has = (me_row > 0, me_row < count_row - 1, me_col > 0, me_col < count_col - 1)
    ids = (
        (me_row - 1, me_col),
        (me_row + 1, me_col),
        (me_row, me_col - 1),
        (me_row, me_col + 1),
    )

    def load(k, b):
        for c in range(tiles):
            pltpu.make_async_copy(
                coef.at[k, b, :, pl.ds(c * LANES, LANES)], planes.at[k, b, c], load_sem.at[k, b]
            ).start()

    def loaded(k, b):
        pltpu.make_async_copy(planes.at[k, b], planes.at[k, b], load_sem.at[k, b]).wait()

    def row_copy(j, b, side):
        h = REACH[j]
        src, dst = (h, h + rows) if side == 0 else (rows, 0)
        return pltpu.make_async_remote_copy(
            src_ref=diff[j].at[b, :, pl.ds(src, h), :],
            dst_ref=diff[j].at[b, :, pl.ds(dst, h), :],
            send_sem=row_send.at[j, b, side],
            recv_sem=row_recv.at[j, b, side],
            device_id=ids[side],
            device_id_type=pl.DeviceIdType.MESH,
        )

    def col_copy(j, b, side):
        return pltpu.make_async_remote_copy(
            src_ref=sent[j].at[b, side],
            dst_ref=got[j].at[b, side],
            send_sem=col_send.at[j, b, side],
            recv_sem=col_recv.at[j, b, side],
            device_id=ids[2 + side],
            device_id_type=pl.DeviceIdType.MESH,
        )

    def start(copy, first, j, b):
        for side in range(2):
            @pl.when(has[first + side])
            def _():
                copy(j, b, side).start()

    def wait(copy, first, j, b):
        for side in range(2):
            @pl.when(has[first + 1 - side])
            def _():
                copy(j, b, side).wait_recv()

    def flush(copy, first, j, b):
        for side in range(2):
            @pl.when(has[first + side])
            def _():
                copy(j, b, side).wait_send()

    def each_bin(f):
        def step(b, carry):
            f(b)
            return carry

        lax.fori_loop(0, bins, step, 0)

    @each_bin
    def _(b):
        load(SCALES, b)
        load(SCALES - 1, b)

    for k in reversed(range(SCALES - 1)):
        each_bin(functools.partial(load, k))

    barrier = pltpu.get_barrier_semaphore()
    for side in range(4):
        @pl.when(has[side])
        def _():
            pl.semaphore_signal(barrier, inc=1, device_id=ids[side], device_id_type=pl.DeviceIdType.MESH)

    for j in range(SCALES):
        h = REACH[j]

        @pl.when(jnp.logical_not(has[0]))
        def _():
            diff[j][:, :, 0:h, :] = jnp.zeros((bins, tiles, h, LANES), jnp.float32)

        @pl.when(jnp.logical_not(has[1]))
        def _():
            diff[j][:, :, h + rows : 2 * h + rows, :] = jnp.zeros((bins, tiles, h, LANES), jnp.float32)

        @pl.when(jnp.logical_not(has[2]))
        def _():
            got[j][:, 1] = jnp.zeros((bins,) + got[j].shape[2:], jnp.float32)

        @pl.when(jnp.logical_not(has[3]))
        def _():
            got[j][:, 0] = jnp.zeros((bins,) + got[j].shape[2:], jnp.float32)

    pl.semaphore_wait(barrier, sum(edge.astype(jnp.int32) for edge in has))

    top = SCALES - 1

    @each_bin
    def _(b):
        loaded(SCALES, b)
        loaded(top, b)
        h = REACH[top]
        for c in range(tiles):
            for r in range(0, rows, 64):
                diff[top][b, c, h + r : h + r + 64, :] = planes[SCALES, b, c, r : r + 64, :] - planes[top, b, c, r : r + 64, :]
        start(row_copy, 0, top, b)

    for j in reversed(range(SCALES)):
        s = STEPS[j]
        h = REACH[j]
        w = REACH[j]
        groups = LANES // w
        part = rows // groups

        @each_bin
        def _(b):
            wait(row_copy, 0, j, b)
            lane = lax.broadcasted_iota(jnp.int32, (part, LANES), 1)
            for c in range(tiles):
                packed = [None, None]
                for g in range(groups):
                    r = h + g * part
                    value = taps(*(diff[j][b, c, r + k * s : r + k * s + part, :] for k in range(-2, 3)))
                    thin[b, c, g * part : (g + 1) * part, :] = value
                    for side in range(2):
                        if c != (0, tiles - 1)[side]:
                            continue
                        turn = (g * w + side * w) % LANES
                        turned = pltpu.roll(value, turn, 1) if turn else value
                        if packed[side] is None:
                            packed[side] = turned
                        else:
                            packed[side] = jnp.where(lane >= g * w, turned, packed[side])
                for side in range(2):
                    if packed[side] is not None:
                        sent[j][b, side] = packed[side]
            start(col_copy, 2, j, b)

        @each_bin
        def _(b):
            wait(col_copy, 2, j, b)
            if j > 0:
                loaded(j - 1, b)
            else:
                pass
            chunk = min(part, 32)
            lane = lax.broadcasted_iota(jnp.int32, (chunk, LANES), 1)
            for r in range(0, rows, chunk):
                g, o = divmod(r, part)
                left = got[j][b, 1, o : o + chunk, :]
                right = got[j][b, 0, o : o + chunk, :]
                x = [thin[b, c, r : r + chunk, :] for c in range(tiles)]

                def turn(v, amount):
                    amount %= LANES
                    return pltpu.roll(v, amount, 1) if amount else v

                shifted = {}
                for d in (s, 2 * s):
                    down = [turn(left, d - g * w - w)] + [turn(v, d) for v in x]
                    up = [turn(v, -d) for v in x] + [turn(right, -g * w - d)]
                    shifted[-d] = [jnp.where(lane < d, down[c], down[c + 1]) for c in range(tiles)]
                    shifted[d] = [jnp.where(lane < LANES - d, up[c], up[c + 1]) for c in range(tiles)]
                for c in range(tiles):
                    total = taps(shifted[-2 * s][c], shifted[-s][c], x[c], shifted[s][c], shifted[2 * s][c])
                    field = planes[j, b, c, r : r + chunk, :] + total * SCALE
                    if j > 0:
                        nxt = REACH[j - 1] + r
                        diff[j - 1][b, c, nxt : nxt + chunk, :] = field - planes[j - 1, b, c, r : r + chunk, :]
                    else:
                        planes[0, b, c, r : r + chunk, :] = field
            if j > 0:
                start(row_copy, 0, j - 1, b)
            else:
                for c in range(tiles):
                    pltpu.make_async_copy(
                        planes.at[0, b, c], out.at[b, :, pl.ds(c * LANES, LANES)], store_sem.at[b]
                    ).start()

    @each_bin
    def _(b):
        pltpu.make_async_copy(planes.at[0, b], planes.at[0, b], store_sem.at[b]).wait()
        for j in range(SCALES):
            flush(row_copy, 0, j, b)
            flush(col_copy, 2, j, b)


def on_device(coefficients, count_row, count_col):
    scales, bins, rows, cols = coefficients.shape
    tiles = cols // LANES
    f32 = jnp.float32
    packed = [pltpu.VMEM((bins, 2, rows * w // LANES, LANES), f32) for w in REACH]
    cells = scales * bins * rows * cols
    return pl.pallas_call(
        functools.partial(body, count_row, count_col),
        out_shape=jax.ShapeDtypeStruct((bins, rows, cols), f32),
        in_specs=[pl.BlockSpec(memory_space=pl.ANY)],
        out_specs=pl.BlockSpec(memory_space=pl.ANY),
        scratch_shapes=[
            pltpu.VMEM((scales, bins, tiles, rows, LANES), f32),
            pltpu.VMEM((bins, tiles, rows, LANES), f32),
            *[pltpu.VMEM((bins, tiles, rows + 2 * h, LANES), f32) for h in REACH],
            *packed,
            *packed,
            pltpu.SemaphoreType.DMA((scales, bins)),
            pltpu.SemaphoreType.DMA((bins,)),
            *[pltpu.SemaphoreType.DMA((SCALES, bins, 2)) for _ in range(4)],
        ],
        compiler_params=pltpu.CompilerParams(
            collective_id=0, has_side_effects=True, vmem_limit_bytes=60 * 2**20
        ),
        cost_estimate=pl.CostEstimate(flops=20 * cells, bytes_accessed=5 * cells, transcendentals=0),
        name="starlet_adjoint",
    )(coefficients)


def solution(mesh):
    return jax.shard_map(
        functools.partial(on_device, count_row=mesh.shape["row"], count_col=mesh.shape["col"]),
        mesh=mesh,
        in_specs=(P(None, None, "row", "col"),),
        out_specs=P(None, "row", "col"),
        check_vma=False,
    )
```

time: 175 us -> 57.2 us (0.33)
  Pallas kernels: 0 us -> 52.2 us
  starting transfers between devices: 50.4 us -> 0 us
  other arithmetic: 49.4 us -> 0 us
  waiting for transfers between devices: 39.5 us -> 0 us
  local copies, waits for them, and re-layouts: 34.7 us -> 4.13 us
    pallas_call x0 -> x1, Pallas kernels: none -> 52.2 us  [on_device(): pl.pallas_call(functools.partial(body, count_row, count_col), out_shape=j...]
    ppermute x20 -> x0, starting transfers between devices: 50.4 us -> none  [the longest x10 25.6 us: with_halo(): lax.ppermute(head, axis, [((i + 1) % count, i) for i in range(ends)])]
    ppermute x20 -> x0, waiting for transfers between devices: 39.5 us -> none  [the longest x10 23.5 us: with_halo(): lax.ppermute(head, axis, [((i + 1) % count, i) for i in range(ends)])]
    sub x5 -> x0, other arithmetic: 32 us -> none  [on_device(): change = field - plane]
    slice x24 -> x0, local copies, waits for them, and re-layouts: 21.9 us -> none  [the longest x17 14.2 us: with_halo(): lax.slice_in_dim(cells, cells.shape[dim] - width, cells.shape[dim], axis=...]
    add x6 -> x0, other arithmetic: 17.4 us -> none  [the longest x5 9.44 us: dilated_filter(): total + TAPS[k] * lax.slice_in_dim(values, k * step, k * step + count, ax...]
    ppermute x14 -> x0, local copies, waits for them, and re-layouts: 12.8 us -> none  [the longest x7 6.82 us: with_halo(): lax.ppermute(head, axis, [((i + 1) % count, i) for i in range(ends)])]
    unnamed x0 -> x1, local copies, waits for them, and re-layouts: none -> 4.13 us
  transfers between devices with their start and end apart: 20 -> 0, of which waited for: 15 -> 0; matrix products, arithmetic and copies ran while one was open for 8% -> 0% of each run, Pallas kernels for 0% -> 0%
where the time goes in v1:
time: 57.2 us; the launch traced here: 56.4 us
  Pallas kernels  52.2 us (91%)
  local copies, waits for them, and re-layouts  4.13 us (7%)
    pallas_call x1, Pallas kernels, on_device(): pl.pallas_call(functools.partial(body, count_row, count_col), out_shape=j...  52.2 us
    unnamed x1, local copies, waits for them, and re-layouts  4.13 us

profile of v1, /device:TPU:4, one launch (start us, length us, event | category | flops | bytes accessed | tf_op | source)
XLA Modules:
  0.0 56.4 jit_solution(14398148447431409350)
XLA Ops:
  0.0 52.2 %starlet_adjoint.1 = f32[6,256,512]{2,1,0:T(8,128)} custom-call(f32[6,6,256,512]{3,2,1,0:T(8,128)} %coef.1), custom_call_target="tpu_custom_call" | custom-call | flops 94371840 | bytes 23592960 | tf_op jit(solution)/shard_map/starlet_adjoint/pallas_call | solution.py:227
  52.2 4.1 %copy.3 = f32[6,256,512]{2,1,0:T(8,128)} copy(f32[6,256,512]{2,1,0:T(8,128)} %starlet_adjoint.1) | data formatting | bytes 6291456

commit v2 on v1

v2 whole, which is shorter than its diff:
```python
import functools

import jax
import jax.numpy as jnp
from jax import lax
from jax.experimental import pallas as pl
from jax.experimental.pallas import tpu as pltpu
from jax.sharding import PartitionSpec as P

SCALES = 5
LANES = 128
WIDE = 256
PARTS = 3
STEPS = tuple(2**j for j in range(SCALES))
REACH = tuple(max(2 * s, 8) for s in STEPS)
SCALE = 1.0 / 256.0


def taps(x0, x1, x2, x3, x4):
    return (x0 + x4) + 4.0 * (x1 + x3) + 6.0 * x2


def split(value):
    parts = []
    for _ in range(PARTS):
        parts.append(value.astype(jnp.bfloat16))
        value = value - parts[-1].astype(jnp.float32)
    return parts


def body(count_row, count_col, coef, out, planes, thin, edge, band, *scratch):
    diff = scratch[:SCALES]
    sent = scratch[SCALES : 2 * SCALES]
    got = scratch[2 * SCALES : 3 * SCALES]
    load_sem, store_sem, row_send, row_recv, col_send, col_recv = scratch[3 * SCALES :]
    bins, rows, cols = planes.shape[1:]
    tiles = cols // LANES
    every = slice(None)

    top = SCALES - 1
    me_row = lax.axis_index("row")
    me_col = lax.axis_index("col")
    has = (me_row > 0, me_row < count_row - 1, me_col > 0, me_col < count_col - 1)
    ids = (
        (me_row - 1, me_col),
        (me_row + 1, me_col),
        (me_row, me_col - 1),
        (me_row, me_col + 1),
    )

    def load(k, b):
        return pltpu.make_async_copy(coef.at[k, b], planes.at[k, b], load_sem.at[k, b])

    def load_all(k):
        return pltpu.make_async_copy(coef.at[k], planes.at[k], load_sem.at[k, 0])

    def store(b):
        return pltpu.make_async_copy(planes.at[0, b], out.at[b], store_sem.at[b])

    def row_copy(j, b, side):
        h = REACH[j]
        src, dst = (h, h + rows) if side == 0 else (rows, 0)
        return pltpu.make_async_remote_copy(
            src_ref=diff[j].at[b, :, pl.ds(src, h), :],
            dst_ref=diff[j].at[b, :, pl.ds(dst, h), :],
            send_sem=row_send.at[j, side],
            recv_sem=row_recv.at[j, 0 if b is every else b, side],
            device_id=ids[side],
            device_id_type=pl.DeviceIdType.MESH,
        )

    def col_copy(j, b, side):
        return pltpu.make_async_remote_copy(
            src_ref=sent[j].at[b, side],
            dst_ref=got[j].at[b, side],
            send_sem=col_send.at[j, side],
            recv_sem=col_recv.at[j, 0 if b is every else b, side],
            device_id=ids[2 + side],
            device_id_type=pl.DeviceIdType.MESH,
        )

    def start(copy, first, j, b):
        for side in range(2):
            @pl.when(has[first + side])
            def _():
                copy(j, b, side).start()

    def wait(copy, first, j, b):
        for side in range(2):
            @pl.when(has[first + 1 - side])
            def _():
                copy(j, b, side).wait_recv()

    def flush(copy, first, j):
        for side in range(2):
            @pl.when(has[first + side])
            def _():
                copy(j, every, side).wait_send()

    def each_bin(f):
        def step(b, carry):
            f(b)
            return carry

        lax.fori_loop(0, bins, step, 0)

    barrier = pltpu.get_barrier_semaphore()
    for side in range(4):
        @pl.when(has[side])
        def _():
            pl.semaphore_signal(barrier, inc=1, device_id=ids[side], device_id_type=pl.DeviceIdType.MESH)

    @each_bin
    def _(b):
        load(SCALES, b).start()
        load(top, b).start()

    for j in range(SCALES):
        h = REACH[j]

        @pl.when(jnp.logical_not(has[0]))
        def _():
            diff[j][:, :, 0:h, :] = jnp.zeros((bins, tiles, h, LANES), jnp.float32)

        @pl.when(jnp.logical_not(has[1]))
        def _():
            diff[j][:, :, h + rows : 2 * h + rows, :] = jnp.zeros((bins, tiles, h, LANES), jnp.float32)

        @pl.when(jnp.logical_not(has[2]))
        def _():
            got[j][:, 1] = jnp.zeros((bins,) + got[j].shape[2:], jnp.float32)

        @pl.when(jnp.logical_not(has[3]))
        def _():
            got[j][:, 0] = jnp.zeros((bins,) + got[j].shape[2:], jnp.float32)

    k = lax.broadcasted_iota(jnp.int32, (WIDE, WIDE), 0)
    n = lax.broadcasted_iota(jnp.int32, (WIDE, WIDE), 1)
    for j in range(SCALES):
        for i, at in enumerate((k, jnp.where(k < LANES, k - LANES, k + LANES))):
            far = jnp.abs(at - n)
            tap = jnp.where(far == 0, 6.0, jnp.where(far == STEPS[j], 4.0, jnp.where(far == 2 * STEPS[j], 1.0, 0.0)))
            for p in range(PARTS):
                row = (i * PARTS + p) * WIDE
                band[j, row : row + WIDE, :] = tap.astype(jnp.bfloat16)

    pl.semaphore_wait(barrier, sum(edge.astype(jnp.int32) for edge in has))

    @each_bin
    def _(b):
        load(SCALES, b).wait()
        load(top, b).wait()
        h = REACH[top]
        for c in range(tiles):
            at = slice(c * LANES, (c + 1) * LANES)
            diff[top][b, c, h : h + rows, :] = planes[SCALES, b, :, at] - planes[top, b, :, at]
        start(row_copy, 0, top, b)

    load_all(top - 1).start()

    def filter_rows(j, b):
        s = STEPS[j]
        h = REACH[j]
        w = REACH[j]
        groups = LANES // w
        part = rows // groups
        wait(row_copy, 0, j, b)
        lane = lax.broadcasted_iota(jnp.int32, (part, LANES), 1)
        for c in range(tiles):
            packed = [None, None]
            for g in range(groups):
                r = h + g * part
                value = taps(*(diff[j][b, c, r + k * s : r + k * s + part, :] for k in range(-2, 3)))
                for p, piece in enumerate(split(value)):
                    thin[b, p, g * part : (g + 1) * part, c * LANES : (c + 1) * LANES] = piece
                for side in range(2):
                    if c != (0, tiles - 1)[side]:
                        continue
                    turn = (g * w + side * w) % LANES
                    turned = pltpu.roll(value, turn, 1) if turn else value
                    if packed[side] is None:
                        packed[side] = turned
                    else:
                        packed[side] = jnp.where(lane >= g * w, turned, packed[side])
            for side in range(2):
                if packed[side] is not None:
                    sent[j][b, side] = packed[side]
        start(col_copy, 2, j, b)

    def filter_cols(j, b):
        s = STEPS[j]
        h = REACH[j]
        w = REACH[j]
        groups = LANES // w
        part = rows // groups
        wait(col_copy, 2, j, b)
        for g in range(groups):
            here = slice(g * part, (g + 1) * part)
            for side in range(2):
                turn = (-g * w - (1 - side) * w) % LANES
                value = got[j][b, 1 - side]
                for p, piece in enumerate(split(pltpu.roll(value, turn, 1) if turn else value)):
                    edge[side, p, here, :] = piece
        blocks = tiles * LANES // WIDE
        for n in range(blocks):
            wide = [thin[b, p, :, n * WIDE : (n + 1) * WIDE] for p in range(PARTS)]
            for p in range(PARTS):
                lo, hi = n * WIDE - LANES, (n + 1) * WIDE
                wide.append(thin[b, p, :, lo : lo + LANES] if n > 0 else edge[0, p])
                wide.append(thin[b, p, :, hi : hi + LANES] if n < blocks - 1 else edge[1, p])
            total = jnp.dot(jnp.concatenate(wide, axis=1), band[j], preferred_element_type=jnp.float32)
            for m in range(WIDE // LANES):
                c = n * (WIDE // LANES) + m
                at = slice(c * LANES, (c + 1) * LANES)
                field = planes[j, b, :, at] + total[:, m * LANES : (m + 1) * LANES] * SCALE
                if j > 0:
                    nxt = REACH[j - 1]
                    diff[j - 1][b, c, nxt : nxt + rows, :] = field - planes[j - 1, b, :, at]
                else:
                    planes[0, b, :, at] = field
        if j > 0:
            start(row_copy, 0, j - 1, b)
        else:
            store(b).start()

    half = bins // 2

    def span(lo, hi, f):
        def step(b, carry):
            f(b)
            return carry

        lax.fori_loop(lo, hi, step, 0)

    span(0, half, lambda b: filter_rows(top, b))
    for j in reversed(range(SCALES)):
        if j > 1:
            load_all(j - 2).start()
        if j > 0:
            load_all(j - 1).wait()

        def ahead(b):
            filter_cols(j, b)
            filter_rows(j, b + half)

        def behind(b):
            filter_cols(j, b + half)
            if j > 0:
                filter_rows(j - 1, b)

        span(0, half, ahead)
        span(0, bins - half, behind)

    for j in reversed(range(SCALES)):
        flush(row_copy, 0, j)
        flush(col_copy, 2, j)

    @each_bin
    def _(b):
        store(b).wait()


def on_device(coefficients, count_row, count_col):
    scales, bins, rows, cols = coefficients.shape
    tiles = cols // LANES
    f32 = jnp.float32
    packed = [pltpu.VMEM((bins, 2, rows * w // LANES, LANES), f32) for w in REACH]
    cells = scales * bins * rows * cols
    return pl.pallas_call(
        functools.partial(body, count_row, count_col),
        out_shape=jax.ShapeDtypeStruct((bins, rows, cols), f32),
        in_specs=[pl.BlockSpec(memory_space=pl.ANY)],
        out_specs=pl.BlockSpec(memory_space=pl.ANY),
        scratch_shapes=[
            pltpu.VMEM((scales, bins, rows, cols), f32),
            pltpu.VMEM((bins, PARTS, rows, cols), jnp.bfloat16),
            pltpu.VMEM((2, PARTS, rows, LANES), jnp.bfloat16),
            pltpu.VMEM((SCALES, 2 * PARTS * WIDE, WIDE), jnp.bfloat16),
            *[pltpu.VMEM((bins, tiles, rows + 2 * h, LANES), f32) for h in REACH],
            *packed,
            *packed,
            pltpu.SemaphoreType.DMA((scales, bins)),
            pltpu.SemaphoreType.DMA((bins,)),
            pltpu.SemaphoreType.DMA((SCALES, 2)),
            pltpu.SemaphoreType.DMA((SCALES, bins, 2)),
            pltpu.SemaphoreType.DMA((SCALES, 2)),
            pltpu.SemaphoreType.DMA((SCALES, bins, 2)),
        ],
        compiler_params=pltpu.CompilerParams(
            collective_id=0, has_side_effects=True, vmem_limit_bytes=60 * 2**20
        ),
        cost_estimate=pl.CostEstimate(flops=20 * cells, bytes_accessed=5 * cells, transcendentals=0),
        name="starlet_adjoint",
    )(coefficients)


def solution(mesh):
    return jax.shard_map(
        functools.partial(on_device, count_row=mesh.shape["row"], count_col=mesh.shape["col"]),
        mesh=mesh,
        in_specs=(P(None, None, "row", "col"),),
        out_specs=P(None, "row", "col"),
        check_vma=False,
    )
```

time: 57.2 us -> 52.9 us (0.925); the launches traced: 56.4 us -> 52.7 us
  Pallas kernels: 52.2 us -> 48.6 us
    pallas_call x1, Pallas kernels: 52.2 us -> 48.6 us  [on_device(): pl.pallas_call(functools.partial(body, count_row, count_col), out_shape=j...]
where the time goes in v2:
time: 52.9 us; the launch traced here: 52.7 us
  Pallas kernels  48.6 us (92%)
  local copies, waits for them, and re-layouts  4.13 us (8%)
    pallas_call x1, Pallas kernels, on_device(): pl.pallas_call(functools.partial(body, count_row, count_col), out_shape=j...  48.6 us
    unnamed x1, local copies, waits for them, and re-layouts  4.13 us

profile of v2, /device:TPU:4, one launch (start us, length us, event | category | flops | bytes accessed | tf_op | source)
XLA Modules:
  0.0 52.7 jit_solution(4110006358168367338)
XLA Ops:
  0.0 48.6 %starlet_adjoint.1 = f32[6,256,512]{2,1,0:T(8,128)} custom-call(f32[6,6,256,512]{3,2,1,0:T(8,128)} %coef.1), custom_call_target="tpu_custom_call" | custom-call | flops 94371840 | bytes 23592960 | tf_op jit(solution)/shard_map/starlet_adjoint/pallas_call | solution.py:269
  48.6 4.1 %copy.3 = f32[6,256,512]{2,1,0:T(8,128)} copy(f32[6,256,512]{2,1,0:T(8,128)} %starlet_adjoint.1) | data formatting | bytes 6291456
